TPU v7x, 512 devices: a whole 4x4x16 slice. The times are simulated.
512 devices in a mesh: fsdp: 16 (over z_lo, core), tp: 32 (over x, y, z_hi).
Axes of the slice: x: 4, y: 4, z: 16 (z_hi: 2, z_lo: 8; z = z_hi * 8 + z_lo), core: 2. Of those that a mesh axis runs over, the one named last changes fastest.
Arguments:
- inputs: bfloat16 [128, 16, 8192], P('tp', None, 'fsdp'), may hold values from -6 to 6
- featurizer: bfloat16 [8192, 3, 8192], P('fsdp', None, 'tp'), may hold values from -0.0625 to 0.0625
- short_filter: float32 [3, 3, 8192], P(None, None, 'tp'), may hold values from -3 to 3
- long_filter: float32 [512, 128], P('tp'), may hold values from -1.2 to 1.2
- decay_rate: float32 [512], P('tp'), may hold values from 0.004 to 0.08
- skip_gain: float32 [8192], P('tp'), may hold values from -1 to 1
- output_grad: bfloat16 [128, 16, 8192], P(None, 'fsdp', 'tp'), may hold values from -6 to 6
Outputs:
- hyena_out: bfloat16 [128, 16, 8192], P(None, 'fsdp', 'tp')
- input_grad: bfloat16 [128, 16, 8192], P('tp', None, 'fsdp')
- weight_grad: bfloat16 [8192, 3, 8192], P('fsdp', None, 'tp')
All inputs are finite; a program needn't handle non-finite values.
Results may differ from a plain program's by a relative error of at most 0.028.
Values may be sent and summed in bfloat16 or wider, within the bound.
No kernel may reach another device: no remote copies, remote signals or barrier semaphores. Data moves between devices by JAX's collectives and lax.ppermute only.
A program may use at most 64 MiB of HBM per device.

v0:
```python
import jax
import jax.numpy as jnp
from jax import lax
from jax.sharding import PartitionSpec as P


def from_behind(x, axis, by):
    devices = lax.axis_size(axis)
    pairs = [(i, i + by) for i in range(devices) if 0 <= i + by < devices]
    return lax.ppermute(x, axis, pairs)


def toeplitz_pair(kernel, tokens):
    tap_count = kernel.shape[1]
    positions = jnp.arange(tokens)
    lag_grid = positions[:, None] - positions[None, :]
    near_inside = (lag_grid >= 0) & (lag_grid < tap_count)
    near_taken = jnp.take(kernel, jnp.clip(lag_grid, 0, tap_count - 1), axis=1)
    near_matrix = jnp.where(near_inside[None], near_taken, jnp.zeros_like(near_taken))
    far_grid = lag_grid + tokens
    far_inside = far_grid < tap_count
    far_taken = jnp.take(kernel, jnp.clip(far_grid, 0, tap_count - 1), axis=1)
    far_matrix = jnp.where(far_inside[None], far_taken, jnp.zeros_like(far_taken))
    return (near_matrix, far_matrix)


def add_sources(pieces):
    return tuple((jnp.sum(member, axis=1) for member in pieces))


def shards(inputs, featurizer, short_filter, long_filter, decay_rate, skip_gain, output_grad):
    gathered = lax.all_gather(inputs, "tp", axis=0, tiled=True)
    tokens, blocks, block_rows = gathered.shape
    halo_rows = short_filter.shape[0] - 1
    channels = featurizer.shape[2]
    wide_columns = 3 * channels
    border = jnp.zeros((halo_rows, 1, block_rows), gathered.dtype)
    earlier_rows = jnp.concatenate([border, gathered[tokens - halo_rows :, : blocks - 1]], axis=1)
    extended = jnp.concatenate([earlier_rows, gathered], axis=0)
    flat_ext = extended.reshape((tokens + halo_rows) * blocks, block_rows)
    partials = [
        jnp.dot(flat_ext, featurizer[:, stream, :], preferred_element_type=jnp.float32).reshape(
            tokens + halo_rows, blocks, channels
        )
        for stream in range(3)
    ]
    summed = add_sources(
        (
            lax.all_to_all(
                partials[0].astype(jnp.bfloat16), "fsdp", split_axis=1, concat_axis=1, tiled=True
            ).astype(jnp.float32),
            lax.all_to_all(
                partials[1].astype(jnp.bfloat16), "fsdp", split_axis=1, concat_axis=1, tiled=True
            ).astype(jnp.float32),
            lax.all_to_all(
                partials[2].astype(jnp.bfloat16), "fsdp", split_axis=1, concat_axis=1, tiled=True
            ).astype(jnp.float32),
        )
    )
    features = jnp.stack([member.astype(jnp.bfloat16) for member in summed], axis=1)
    feat_wide = features.astype(jnp.float32)
    filtered = short_filter[0] * feat_wide[halo_rows:]
    for lag_step in range(1, halo_rows + 1):
        filtered = (
            filtered
            + short_filter[lag_step]
            * feat_wide[halo_rows - lag_step : halo_rows - lag_step + tokens]
        )
    queries = filtered[:, 0]
    key_part = filtered[:, 1]
    value_part = filtered[:, 2]
    product = key_part * value_part
    offsets = jnp.arange(long_filter.shape[1]).astype(jnp.float32)
    kernel = long_filter * jnp.exp(-decay_rate[:, None] * offsets[None, :])
    near_matrix, far_matrix = toeplitz_pair(kernel, tokens)
    filter_count = kernel.shape[0]
    group_width = channels // filter_count
    grouped = product.reshape(tokens, filter_count, group_width)
    local_conv = jnp.einsum(
        "nst,tnc->snc", near_matrix, grouped, precision=lax.Precision.HIGHEST
    ).reshape(tokens, channels)
    earlier = from_behind(product.astype(jnp.bfloat16), "fsdp", 1).astype(product.dtype)
    far_conv = jnp.einsum(
        "nst,tnc->snc",
        far_matrix,
        earlier.reshape(tokens, filter_count, group_width),
        precision=lax.Precision.HIGHEST,
    ).reshape(tokens, channels)
    convolved = local_conv + far_conv + skip_gain * product
    hyena_out = (queries * convolved).astype(jnp.bfloat16).reshape(tokens, 1, channels)
    upstream = output_grad.reshape(tokens, channels).astype(jnp.float32)
    query_grad = upstream * convolved
    conv_grad = upstream * queries
    conv_grouped = conv_grad.reshape(tokens, filter_count, group_width)
    local_back = jnp.einsum(
        "nst,snc->tnc", near_matrix, conv_grouped, precision=lax.Precision.HIGHEST
    ).reshape(tokens, channels)
    later_grad = from_behind(conv_grad.astype(jnp.bfloat16), "fsdp", -1).astype(conv_grad.dtype)
    far_back = jnp.einsum(
        "nst,snc->tnc",
        far_matrix,
        later_grad.reshape(tokens, filter_count, group_width),
        precision=lax.Precision.HIGHEST,
    ).reshape(tokens, channels)
    product_grad = local_back + far_back + skip_gain * conv_grad
    filtered_grad = jnp.stack(
        [query_grad, product_grad * value_part, product_grad * key_part], axis=1
    )
    next_head = from_behind(filtered_grad[:halo_rows], "fsdp", -1)
    padded = jnp.concatenate([filtered_grad, next_head], axis=0)
    feature_grad = short_filter[0] * filtered_grad
    for lag_step in range(1, halo_rows + 1):
        feature_grad = feature_grad + short_filter[lag_step] * padded[lag_step : lag_step + tokens]
    grad_own = feature_grad.astype(jnp.bfloat16).reshape(tokens, 1, wide_columns)
    grad_all = lax.all_gather(grad_own, "fsdp", axis=1, tiled=True)
    weight_block = featurizer.reshape(block_rows, wide_columns)
    weight_grad = lax.dot_general(
        gathered, grad_all, (((0, 1), (0, 1)), ((), ())), preferred_element_type=jnp.float32
    )
    weight_grad = weight_grad.astype(jnp.bfloat16).reshape(featurizer.shape)
    own_count = tokens // lax.axis_size("tp")
    flat_piece = grad_all.reshape(own_count * lax.axis_size("tp") * blocks, wide_columns)
    result = lax.dot_general(
        flat_piece, weight_block, (((1,), (1,)), ((), ())), preferred_element_type=jnp.float32
    )
    input_grad = lax.psum_scatter(
        result.reshape(own_count * lax.axis_size("tp"), blocks, block_rows).astype(jnp.bfloat16),
        "tp",
        scatter_dimension=0,
        tiled=True,
    )
    return (hyena_out, input_grad, weight_grad)


def solution(mesh):
    in_specs = (
        P("tp", None, "fsdp"),
        P("fsdp", None, "tp"),
        P(None, None, "tp"),
        P("tp", None),
        P("tp"),
        P("tp"),
        P(None, "fsdp", "tp"),
    )
    out_specs = (P(None, "fsdp", "tp"), P("tp", None, "fsdp"), P("fsdp", None, "tp"))
    return jax.shard_map(shards, mesh=mesh, in_specs=in_specs, out_specs=out_specs, check_vma=False)
```

profile of v0, /device:TPU:4, one launch (start us, length us, event | category | flops | bytes accessed | tf_op | source)
XLA Modules:
  0.0 920.4 jit_solution(7407251781027713006)
XLA Ops:
  7.2 0.0 all-gather.3.cloned.1.call-start
  7.2 0.7 all-gather.3.cloned.1.call-update
  7.9 139.1 %all-gather.3.cloned.1.call-done = bf16[128,16,512]{2,1,0:T(8,128)(2,1)} async-done(((bf16[4,16,512]{2,1,0:T(8,128)(2,1)}), bf16[128,16,512]{2,1,0:T(8,128)(2,1)}) %all-gather.3.cloned.1.call-update) | async-done | bytes 2097168 | tf_op jit(solution)/shard_map/all_gather | solution.py:32
  147.0 0.8 slice.71
  147.8 2.3 convolution_convert_fusion.3
  150.1 0.0 copy-start.1
  150.1 1.4 copy.59
  151.4 3.7 all-to-all-start
  155.2 0.0 copy-done.1
  155.2 2.3 convolution_convert_fusion.2
  157.5 1.4 copy.61
  158.9 42.5 %all-to-all-done = bf16[130,16,256]{2,0,1:T(8,128)(2,1)S(1)} async-done(((bf16[130,16,256]{2,0,1:T(8,128)(2,1)}), bf16[130,16,256]{2,0,1:T(8,128)(2,1)S(1)}, u32[]{:S(2)}, u32[]{:S(2)}) %all-to-all-start) | async-done | bytes 1064992 | tf_op jit(solution)/shard_map/all_to_all | solution.py:49
  201.3 11.8 %all-to-all-start.1 = ((bf16[130,16,256]{2,0,1:T(8,128)(2,1)}), bf16[130,16,256]{2,0,1:T(8,128)(2,1)S(1)}, u32[]{:S(2)}, u32[]{:S(2)}) async-start(bf16[130,16,256]{2,0,1:T(8,128)(2,1)} %copy.61), calls=%async_computation.1 | async-start | bytes 2228224 | tf_op jit(solution)/shard_map/all_to_all | solution.py:52
  213.1 2.3 convolution_convert_fusion.1
  215.4 0.0 copy-start.8
  215.4 0.0 copy-start.5
  215.4 1.4 copy.63
  216.8 42.5 %all-to-all-done.1 = bf16[130,16,256]{2,0,1:T(8,128)(2,1)S(1)} async-done(((bf16[130,16,256]{2,0,1:T(8,128)(2,1)}), bf16[130,16,256]{2,0,1:T(8,128)(2,1)S(1)}, u32[]{:S(2)}, u32[]{:S(2)}) %all-to-all-start.1) | async-done | bytes 1064992 | tf_op jit(solution)/shard_map/all_to_all | solution.py:52
  259.3 11.8 %all-to-all-start.2 = ((bf16[130,16,256]{2,0,1:T(8,128)(2,1)}), bf16[130,16,256]{2,0,1:T(8,128)(2,1)}, u32[]{:S(2)}, u32[]{:S(2)}) async-start(bf16[130,16,256]{2,0,1:T(8,128)(2,1)} %copy.63), calls=%async_computation.2 | async-start | bytes 2228224 | tf_op jit(solution)/shard_map/all_to_all | solution.py:55
  271.1 0.0 all-gather.5.cloned.1.call-start
  271.2 0.1 exponential_multiply_fusion
  271.3 0.1 copy.66
  271.4 54.8 %gather_fusion = f32[16384,16]{1,0:T(8,128)} fusion(f32[16,128]{0,1:T(8,128)S(1)} %copy.66, s32[16384]{0:T(1024)S(1)} %bitcast_clamp_fusion.1), kind=kCustom, calls=%fused_computation.clone | custom fusion | bytes 2162688 | tf_op jit(solution)/shard_map/jit(_take)/gather | solution.py:18
  326.2 5.2 copy.67
  331.5 54.8 %gather_fusion.1 = f32[16384,16]{1,0:T(8,128)} fusion(f32[16,128]{0,1:T(8,128)S(1)} %copy.66, s32[16384]{0:T(1024)S(1)} %bitcast_clamp_fusion), kind=kCustom, calls=%fused_computation.1.clone | custom fusion | bytes 2162688 | tf_op jit(solution)/shard_map/jit(_take)/gather | solution.py:22
  386.3 5.2 copy.70
  391.7 0.2 reduce_sum.36
  391.8 0.0 copy-start.3
  391.8 1.4 reduce_sum.37
  393.3 0.0 all-to-all-done.2
  393.3 1.4 reduce_sum.38
  394.7 0.1 fusion.27
  394.9 0.0 copy-done.3
  394.9 0.1 copy.65
  395.0 2.3 collective-permute-start
  397.3 0.1 copy.72
  397.4 1.7 fusion.7
  399.1 1.0 fusion.6
  400.2 1.4 collective-permute-start.1
  401.6 0.0 collective-permute-done
  401.6 0.1 copy.68
  401.7 1.0 convolution_add_fusion.1
  402.7 0.1 copy.71
  402.8 1.8 collective-permute-done.1
  404.6 0.1 copy.73
  404.7 0.7 convolution_add_fusion
  405.4 0.1 copy.74
  405.5 0.7 slice_multiply_fusion.5
  406.2 1.4 collective-permute-start.2
  407.7 4.2 collective-permute-done.2
  411.9 0.1 fusion.25
  412.1 0.2 copy.75
  412.2 0.8 copy.76
  413.1 0.0 all-gather.5.cloned.1.call-update
  413.1 0.2 reduce-scatter.2.cloned.1.call-start
  413.3 0.0 copy-done.2
  413.3 0.3 copy.77
  413.6 102.8 %all-gather.5.cloned.1.call-done = bf16[128,16,768]{2,0,1:T(8,128)(2,1)} async-done(((bf16[128,1,768]{2,0,1:T(8,128)(2,1)}), bf16[128,16,768]{2,0,1:T(8,128)(2,1)}) %all-gather.5.cloned.1.call-update) | async-done | bytes 3145744 | tf_op jit(solution)/shard_map/all_gather | solution.py:115
  516.4 3.7 convolution_convert_fusion
  520.1 2.5 copy.79
  522.7 0.0 reduce-scatter.2.cloned.1.call-update
  522.7 5.3 bitcast_convert_fusion
  528.0 1.2 copy.82
  529.2 384.7 %reduce-scatter.2.cloned.1.call-done = bf16[4,16,512]{2,1,0:T(8,128)(2,1)} async-done(((bf16[128,16,512]{2,1,0:T(8,128)(2,1)}), bf16[4,16,512]{2,1,0:T(8,128)(2,1)}) %reduce-scatter.2.cloned.1.call-update) | async-done | bytes 65552 | tf_op jit(solution)/shard_map/reduce_scatter | solution.py:126
  (23 shorter events, 0.3 us)
Async XLA Ops:
  7.2 139.8 %all-gather.3.cloned.1.call-start = ((), (), s32[]{:S(2)}) async-start(), calls=%async_computation.4 | async-start | bytes 2162688 | tf_op jit(solution)/shard_map/all_gather | solution.py:32
  150.1 5.1 copy-start.1
  151.4 49.9 %all-to-all-start = ((bf16[130,16,256]{2,0,1:T(8,128)(2,1)}), bf16[130,16,256]{2,0,1:T(8,128)(2,1)S(1)}, u32[]{:S(2)}, u32[]{:S(2)}) async-start(bf16[130,16,256]{2,0,1:T(8,128)(2,1)} %copy.59), calls=%async_computation | async-start | bytes 2228224 | tf_op jit(solution)/shard_map/all_to_all | solution.py:49
  201.3 58.0 %all-to-all-start.1 = ((bf16[130,16,256]{2,0,1:T(8,128)(2,1)}), bf16[130,16,256]{2,0,1:T(8,128)(2,1)S(1)}, u32[]{:S(2)}, u32[]{:S(2)}) async-start(bf16[130,16,256]{2,0,1:T(8,128)(2,1)} %copy.61), calls=%async_computation.1 | async-start | bytes 2228224 | tf_op jit(solution)/shard_map/all_to_all | solution.py:52
  215.4 55.7 %copy-start.8 = (f32[16]{0:T(128)S(1)}, f32[16]{0:T(128)}, u32[]{:S(2)}) copy-start(f32[16]{0:T(128)} %param.13) | copy-start | bytes 196
  215.4 55.8 %copy-start.5 = (f32[16,128]{1,0:T(8,128)S(1)}, f32[16,128]{1,0:T(8,128)}, u32[]{:S(2)}) copy-start(f32[16,128]{1,0:T(8,128)} %param.12) | copy-start | bytes 24580
  259.3 11.9 %copy-start = (bf16[130,16,256]{2,0,1:T(8,128)(2,1)}, bf16[130,16,256]{2,0,1:T(8,128)(2,1)S(1)}, u32[]{:S(2)}) copy-start(bf16[130,16,256]{2,0,1:T(8,128)(2,1)S(1)} %all-to-all-done.1) | copy-start | bytes 3194884
  259.3 134.0 %all-to-all-start.2 = ((bf16[130,16,256]{2,0,1:T(8,128)(2,1)}), bf16[130,16,256]{2,0,1:T(8,128)(2,1)}, u32[]{:S(2)}, u32[]{:S(2)}) async-start(bf16[130,16,256]{2,0,1:T(8,128)(2,1)} %copy.63), calls=%async_computation.2 | async-start | bytes 2228224 | tf_op jit(solution)/shard_map/all_to_all | solution.py:55
  271.1 245.4 %all-gather.5.cloned.1.call-start = ((), (), s32[]{:S(2)}) async-start(), calls=%async_computation.5 | async-start | bytes 3342336 | tf_op jit(solution)/shard_map/all_gather | solution.py:115
  386.3 5.3 copy-start.4
  391.8 3.0 copy-start.3
  395.0 6.6 collective-permute-start
  400.2 5.3 copy-start.6
  400.2 4.4 collective-permute-start.1
  406.2 7.1 copy-start.2
  406.2 5.6 collective-permute-start.2
  413.1 500.8 %reduce-scatter.2.cloned.1.call-start = ((), (), s32[]{:S(2)}) async-start(), calls=%async_computation.6 | async-start | bytes 2162688 | tf_op jit(solution)/shard_map/reduce_scatter | solution.py:126
  520.1 2.6 copy-start.7
Sparse Core Ops, SparseCore 0:
  12.3 134.6 all-gather.2
  413.2 103.1 all-gather.4
  522.8 391.0 reduce-scatter.1
where the time goes:
time: 921 us; the launch traced here: 920 us
  waiting for transfers between devices  718 us (78%)
  local copies, waits for them, and re-layouts  131 us (14%)
  starting transfers between devices  32.6 us (4%)
  matrix products  20.3 us (2%)
  between operations  14.1 us (2%)
    reduce_scatter x1, waiting for transfers between devices, shards(): lax.psum_scatter(result.reshape(own_count * lax.axis_size('tp'), blocks,...  385 us
    all_gather x1, waiting for transfers between devices, shards(): gathered = lax.all_gather(inputs, 'tp', axis=0, tiled=True)  139 us
    all_gather x1, waiting for transfers between devices, shards(): grad_all = lax.all_gather(grad_own, 'fsdp', axis=1, tiled=True)  103 us
    gather x2, local copies, waits for them, and re-layouts, toeplitz_pair(): far_taken = jnp.take(kernel, jnp.clip(far_grid, 0, tap_count - 1), axis=1)  60 us
    gather x2, local copies, waits for them, and re-layouts, toeplitz_pair(): near_taken = jnp.take(kernel, jnp.clip(lag_grid, 0, tap_count - 1), axis=1)  60 us
    all_to_all x1, waiting for transfers between devices, shards(): lax.all_to_all(partials[1].astype(jnp.bfloat16), 'fsdp', split_axis=1, co...  42.5 us
    all_to_all x1, waiting for transfers between devices, shards(): lax.all_to_all(partials[0].astype(jnp.bfloat16), 'fsdp', split_axis=1, co...  42.5 us
  transfers between devices with their start and end apart: 9, of which 7 were waited for; matrix products, arithmetic and copies ran while one was open for 15% of the time, Pallas kernels for 0%

commit v1 on v0

--- a/solution.py
+++ b/solution.py
@@ -112,7 +112,10 @@
     for lag_step in range(1, halo_rows + 1):
         feature_grad = feature_grad + short_filter[lag_step] * padded[lag_step : lag_step + tokens]
     grad_own = feature_grad.astype(jnp.bfloat16).reshape(tokens, 1, wide_columns)
-    grad_all = lax.all_gather(grad_own, "fsdp", axis=1, tiled=True)
+    count = lax.axis_size("fsdp")
+    parts = jnp.stack([grad_own for _ in range(count)])
+    parts = lax.all_to_all(parts, "fsdp", split_axis=0, concat_axis=0)
+    grad_all = jnp.concatenate(parts, axis=1)
     weight_block = featurizer.reshape(block_rows, wide_columns)
     weight_grad = lax.dot_general(
         gathered, grad_all, (((0, 1), (0, 1)), ((), ())), preferred_element_type=jnp.float32

time: 921 us -> 975 us (1.059)
  the two profiles are of different devices: /device:TPU:4 before, /device:TPU:32 now
where the time goes in v1:
time: 975 us; the launch traced here: 974 us
  waiting for transfers between devices  747 us (77%)
  local copies, waits for them, and re-layouts  134 us (14%)
  starting transfers between devices  53.3 us (5%)
  matrix products  20.2 us (2%)
  between operations  14.4 us (1%)
    reduce_scatter x1, waiting for transfers between devices, shards(): lax.psum_scatter(result.reshape(own_count * lax.axis_size('tp'), blocks,...  396 us
    all_gather x1, waiting for transfers between devices, shards(): gathered = lax.all_gather(inputs, 'tp', axis=0, tiled=True)  134 us
    all_to_all x1, waiting for transfers between devices, shards(): parts = lax.all_to_all(parts, 'fsdp', split_axis=0, concat_axis=0)  129 us
    gather x2, local copies, waits for them, and re-layouts, toeplitz_pair(): far_taken = jnp.take(kernel, jnp.clip(far_grid, 0, tap_count - 1), axis=1)  59.7 us
    gather x2, local copies, waits for them, and re-layouts, toeplitz_pair(): near_taken = jnp.take(kernel, jnp.clip(lag_grid, 0, tap_count - 1), axis=1)  59.7 us
    all_to_all x1, waiting for transfers between devices, shards(): lax.all_to_all(partials[0].astype(jnp.bfloat16), 'fsdp', split_axis=1, co...  42.7 us
    all_to_all x1, waiting for transfers between devices, shards(): lax.all_to_all(partials[1].astype(jnp.bfloat16), 'fsdp', split_axis=1, co...  42.6 us
  transfers between devices with their start and end apart: 9, of which 7 were waited for; matrix products, arithmetic and copies ran while one was open for 15% of the time, Pallas kernels for 0%

profile of v1, /device:TPU:32, one launch (start us, length us, event | category | flops | bytes accessed | tf_op | source)
XLA Modules:
  0.0 973.8 jit_solution(2551921548365953898)
XLA Ops:
  7.2 0.0 all-gather.2.cloned.1.call-start
  7.2 0.7 all-gather.2.cloned.1.call-update
  7.9 134.1 %all-gather.2.cloned.1.call-done = bf16[128,16,512]{2,1,0:T(8,128)(2,1)} async-done(((bf16[4,16,512]{2,1,0:T(8,128)(2,1)}), bf16[128,16,512]{2,1,0:T(8,128)(2,1)}) %all-gather.2.cloned.1.call-update) | async-done | bytes 2097168 | tf_op jit(solution)/shard_map/all_gather | solution.py:32
  142.0 0.8 slice.71
  142.7 2.3 convolution_convert_fusion.2
  145.0 0.0 copy-start.1
  145.0 1.4 copy.59
  146.4 10.2 %all-to-all-start = ((bf16[130,16,256]{2,0,1:T(8,128)(2,1)}), bf16[130,16,256]{2,0,1:T(8,128)(2,1)S(1)}, u32[]{:S(2)}, u32[]{:S(2)}) async-start(bf16[130,16,256]{2,0,1:T(8,128)(2,1)} %copy.59), calls=%async_computation | async-start | bytes 2228224 | tf_op jit(solution)/shard_map/all_to_all | solution.py:49
  156.6 0.0 copy-done.1
  156.6 2.3 convolution_convert_fusion.1
  158.9 1.4 copy.61
  160.3 42.7 %all-to-all-done = bf16[130,16,256]{2,0,1:T(8,128)(2,1)S(1)} async-done(((bf16[130,16,256]{2,0,1:T(8,128)(2,1)}), bf16[130,16,256]{2,0,1:T(8,128)(2,1)S(1)}, u32[]{:S(2)}, u32[]{:S(2)}) %all-to-all-start) | async-done | bytes 1064992 | tf_op jit(solution)/shard_map/all_to_all | solution.py:49
  203.0 11.6 %all-to-all-start.1 = ((bf16[130,16,256]{2,0,1:T(8,128)(2,1)}), bf16[130,16,256]{2,0,1:T(8,128)(2,1)S(1)}, u32[]{:S(2)}, u32[]{:S(2)}) async-start(bf16[130,16,256]{2,0,1:T(8,128)(2,1)} %copy.61), calls=%async_computation.1 | async-start | bytes 2228224 | tf_op jit(solution)/shard_map/all_to_all | solution.py:52
  214.7 2.3 convolution_convert_fusion
  217.0 0.0 copy-start.6
  217.0 0.0 copy-start.4
  217.0 1.4 copy.63
  218.4 42.6 %all-to-all-done.1 = bf16[130,16,256]{2,0,1:T(8,128)(2,1)S(1)} async-done(((bf16[130,16,256]{2,0,1:T(8,128)(2,1)}), bf16[130,16,256]{2,0,1:T(8,128)(2,1)S(1)}, u32[]{:S(2)}, u32[]{:S(2)}) %all-to-all-start.1) | async-done | bytes 1064992 | tf_op jit(solution)/shard_map/all_to_all | solution.py:52
  261.0 11.6 %all-to-all-start.2 = ((bf16[130,16,256]{2,0,1:T(8,128)(2,1)}), bf16[130,16,256]{2,0,1:T(8,128)(2,1)}, u32[]{:S(2)}, u32[]{:S(2)}) async-start(bf16[130,16,256]{2,0,1:T(8,128)(2,1)} %copy.63), calls=%async_computation.2 | async-start | bytes 2228224 | tf_op jit(solution)/shard_map/all_to_all | solution.py:55
  272.6 0.0 copy-done.6
  272.7 0.1 exponential_multiply_fusion
  272.7 0.1 copy.66
  272.9 54.5 %gather_fusion = f32[16384,16]{1,0:T(8,128)} fusion(f32[16,128]{0,1:T(8,128)S(1)} %copy.66, s32[16384]{0:T(1024)S(1)} %bitcast_clamp_fusion.1), kind=kCustom, calls=%fused_computation.clone | custom fusion | bytes 2162688 | tf_op jit(solution)/shard_map/jit(_take)/gather | solution.py:18
  327.4 5.2 copy.67
  332.6 54.5 %gather_fusion.1 = f32[16384,16]{1,0:T(8,128)} fusion(f32[16,128]{0,1:T(8,128)S(1)} %copy.66, s32[16384]{0:T(1024)S(1)} %bitcast_clamp_fusion), kind=kCustom, calls=%fused_computation.1.clone | custom fusion | bytes 2162688 | tf_op jit(solution)/shard_map/jit(_take)/gather | solution.py:22
  387.2 5.2 copy.70
  392.5 0.2 reduce_sum.36
  392.7 0.0 copy-start.2
  392.7 1.4 reduce_sum.37
  394.1 0.0 all-to-all-done.2
  394.1 1.4 reduce_sum.38
  395.6 0.1 fusion.35
  395.8 0.1 copy.65
  395.9 2.0 collective-permute-start
  397.9 0.1 copy.72
  398.0 1.7 fusion.15
  399.7 1.0 fusion.14
  400.8 3.7 collective-permute-start.1
  404.5 0.0 collective-permute-done
  404.5 0.1 copy.68
  404.6 1.0 convolution_add_fusion.1
  405.6 0.1 copy.71
  405.7 0.7 collective-permute-done.1
  406.3 0.1 copy.73
  406.5 0.7 convolution_add_fusion
  407.2 0.1 copy.74
  407.3 0.0 copy-done.5
  407.3 0.7 slice_multiply_fusion.5
  408.0 3.7 collective-permute-start.2
  411.7 1.3 collective-permute-done.2
  413.1 0.1 fusion.33
  413.2 0.2 copy.75
  413.4 0.2 copy.76
  413.5 2.0 stack.26
  415.5 10.2 %all-to-all-start.3 = ((bf16[16,128,1,768]{3,1,2,0:T(8,128)(2,1)}), bf16[16,128,1,768]{3,1,2,0:T(8,128)(2,1)S(1)}, u32[]{:S(2)}, u32[]{:S(2)}) async-start(bf16[16,128,1,768]{3,1,2,0:T(8,128)(2,1)} %stack.26), calls=%async_computation.3 | async-start | bytes 6291456 | tf_op jit(solution)/shard_map/all_to_all | solution.py:117
  425.7 0.2 reduce-scatter.2.cloned.1.call-start
  425.9 2.3 copy.78
  428.2 129.1 %all-to-all-done.3 = bf16[16,128,1,768]{3,1,2,0:T(8,128)(2,1)S(1)} async-done(((bf16[16,128,1,768]{3,1,2,0:T(8,128)(2,1)}), bf16[16,128,1,768]{3,1,2,0:T(8,128)(2,1)S(1)}, u32[]{:S(2)}, u32[]{:S(2)}) %all-to-all-start.3) | async-done | bytes 3145760 | tf_op jit(solution)/shard_map/all_to_all | solution.py:117
  557.3 2.9 fusion.7
  560.2 2.5 copy.80
  562.7 0.0 reduce-scatter.2.cloned.1.call-update
  562.7 5.9 bitcast_convert_fusion
  568.6 2.3 copy.83
  570.9 396.1 %reduce-scatter.2.cloned.1.call-done = bf16[4,16,512]{2,1,0:T(8,128)(2,1)} async-done(((bf16[128,16,512]{2,1,0:T(8,128)(2,1)}), bf16[4,16,512]{2,1,0:T(8,128)(2,1)}) %reduce-scatter.2.cloned.1.call-update) | async-done | bytes 65552 | tf_op jit(solution)/shard_map/reduce_scatter | solution.py:129
  (19 shorter events, 0.3 us)
Async XLA Ops:
  7.2 134.8 %all-gather.2.cloned.1.call-start = ((), (), s32[]{:S(2)}) async-start(), calls=%async_computation.5 | async-start | bytes 2162688 | tf_op jit(solution)/shard_map/all_gather | solution.py:32
  145.0 11.6 %copy-start.1 = (bf16[512,3,256]{2,0,1:T(8,128)(2,1)S(1)}, bf16[512,3,256]{2,0,1:T(8,128)(2,1)}, u32[]{:S(2)}) copy-start(bf16[512,3,256]{2,0,1:T(8,128)(2,1)} %param.10) | copy-start | bytes 2359300
  146.4 56.6 %all-to-all-start = ((bf16[130,16,256]{2,0,1:T(8,128)(2,1)}), bf16[130,16,256]{2,0,1:T(8,128)(2,1)S(1)}, u32[]{:S(2)}, u32[]{:S(2)}) async-start(bf16[130,16,256]{2,0,1:T(8,128)(2,1)} %copy.59), calls=%async_computation | async-start | bytes 2228224 | tf_op jit(solution)/shard_map/all_to_all | solution.py:49
  203.0 58.0 %all-to-all-start.1 = ((bf16[130,16,256]{2,0,1:T(8,128)(2,1)}), bf16[130,16,256]{2,0,1:T(8,128)(2,1)S(1)}, u32[]{:S(2)}, u32[]{:S(2)}) async-start(bf16[130,16,256]{2,0,1:T(8,128)(2,1)} %copy.61), calls=%async_computation.1 | async-start | bytes 2228224 | tf_op jit(solution)/shard_map/all_to_all | solution.py:52
  217.0 55.6 %copy-start.6 = (f32[16]{0:T(128)S(1)}, f32[16]{0:T(128)}, u32[]{:S(2)}) copy-start(f32[16]{0:T(128)} %param.13) | copy-start | bytes 196
  217.0 55.7 %copy-start.4 = (f32[16,128]{1,0:T(8,128)S(1)}, f32[16,128]{1,0:T(8,128)}, u32[]{:S(2)}) copy-start(f32[16,128]{1,0:T(8,128)} %param.12) | copy-start | bytes 24580
  261.0 11.6 %copy-start = (bf16[130,16,256]{2,0,1:T(8,128)(2,1)}, bf16[130,16,256]{2,0,1:T(8,128)(2,1)S(1)}, u32[]{:S(2)}) copy-start(bf16[130,16,256]{2,0,1:T(8,128)(2,1)S(1)} %all-to-all-done.1) | copy-start | bytes 3194884
  261.0 133.1 %all-to-all-start.2 = ((bf16[130,16,256]{2,0,1:T(8,128)(2,1)}), bf16[130,16,256]{2,0,1:T(8,128)(2,1)}, u32[]{:S(2)}, u32[]{:S(2)}) async-start(bf16[130,16,256]{2,0,1:T(8,128)(2,1)} %copy.63), calls=%async_computation.2 | async-start | bytes 2228224 | tf_op jit(solution)/shard_map/all_to_all | solution.py:55
  387.2 5.3 copy-start.3
  392.7 3.0 copy-start.2
  395.9 8.6 collective-permute-start
  400.8 6.5 copy-start.5
  400.8 5.6 collective-permute-start.1
  408.0 5.0 collective-permute-start.2
  415.5 141.8 %all-to-all-start.3 = ((bf16[16,128,1,768]{3,1,2,0:T(8,128)(2,1)}), bf16[16,128,1,768]{3,1,2,0:T(8,128)(2,1)S(1)}, u32[]{:S(2)}, u32[]{:S(2)}) async-start(bf16[16,128,1,768]{3,1,2,0:T(8,128)(2,1)} %stack.26), calls=%async_computation.3 | async-start | bytes 6291456 | tf_op jit(solution)/shard_map/all_to_all | solution.py:117
  425.7 541.3 %reduce-scatter.2.cloned.1.call-start = ((), (), s32[]{:S(2)}) async-start(), calls=%async_computation.6 | async-start | bytes 2162688 | tf_op jit(solution)/shard_map/reduce_scatter | solution.py:129
Sparse Core Ops, SparseCore 0:
  12.3 129.6 all-gather.1
  562.9 404.0 reduce-scatter.1
